TPU v7x, 32 devices: a whole 2x2x4 slice. The times are simulated.
32 devices in a mesh: dp: 8 (over y, x, core), tensor: 4 (over z).
Axes of the slice: x: 2, y: 2, z: 4, core: 2. Of those that a mesh axis runs over, the one named last changes fastest.
Arguments:
- tokens: bfloat16 [16384, 1024], P(('dp', 'tensor')), may hold values from -6 to 6
- cotangent: bfloat16 [16384, 1024], P(('dp', 'tensor')), may hold values from -6 to 6
- lengths: int32 [32], replicated, may hold values from 1 to 1024, as said below
- deal: int32 [32], replicated, may hold values from 0 to 31, as said below
- w_qkv: bfloat16 [3, 1024, 1024], P(None, 'dp', 'tensor'), may hold values from -0.1875 to 0.1875
- w_o: bfloat16 [1024, 1024], P('tensor', 'dp'), may hold values from -0.1875 to 0.1875
- w_1: bfloat16 [1024, 4096], P('dp', 'tensor'), may hold values from -0.1875 to 0.1875
- w_2: bfloat16 [4096, 1024], P('tensor', 'dp'), may hold values from -0.09375 to 0.09375
- b_qv: float32 [2, 1024], P(None, 'tensor'), may hold values from -1.8 to 1.8
- b_o: float32 [1024], replicated, may hold values from -0.3 to 0.3
- b_1: float32 [4096], P('tensor'), may hold values from -1.8 to 1.8
- b_2: float32 [1024], replicated, may hold values from -1.2 to 1.2
- ln_gain: float32 [4, 1024], replicated, may hold values from 0.25 to 1.75
- ln_bias: float32 [4, 1024], replicated, may hold values from -1.8 to 1.8
Outputs:
- output: bfloat16 [16384, 1024], P(('dp', 'tensor'))
- input_grad: bfloat16 [16384, 1024], P(('dp', 'tensor'))
- w_qkv_grad: float32 [3, 1024, 1024], P(None, 'dp', 'tensor')
- w_o_grad: float32 [1024, 1024], P('tensor', 'dp')
- w_1_grad: float32 [1024, 4096], P('dp', 'tensor')
- w_2_grad: float32 [4096, 1024], P('tensor', 'dp')
- b_qv_grad: float32 [2, 1024], P(None, 'tensor')
- b_o_grad: float32 [1024], replicated
- b_1_grad: float32 [4096], P('tensor')
- b_2_grad: float32 [1024], replicated
- ln_gain_grad: float32 [4, 1024], replicated
- ln_bias_grad: float32 [4, 1024], replicated
Inputs may be any that keep to these rules, and one draw needn't show every extreme that they name: The 4 sequences that deal gives to one data group have lengths that sum to 2048, and one of them has exactly 1024 tokens. `deal`: A permutation of the sequences; slots b * 4 to b * 4 + 3 belong to data group b.
All inputs are finite; a program needn't handle non-finite values. Where the computation divides by a largest or mean magnitude, that divisor is 1e-20 or more.
Results may differ from a plain program's by a relative error of at most 0.015.
Values may be sent and summed in bfloat16 or wider, within the bound.
A program may use at most 192 MiB of HBM per device.

v0:
```python
from functools import partial
import math
import jax
import jax.numpy as jnp
from jax import lax
from jax.sharding import PartitionSpec as P

DH = 64
MAXLEN = 1024
QBLK = 512
NORM_EPS = 1e-05
RELAX_FACTOR = 32.0
MASKED_OUT = -1000000000.0


def scaled_norm(values, norm_gain, norm_shift):
    peak = jnp.max(jnp.abs(values), axis=-1, keepdims=True) + NORM_EPS
    scaled = values / peak
    centred = scaled - jnp.mean(scaled, axis=-1, keepdims=True)
    spread = jnp.mean(centred * centred, axis=-1, keepdims=True)
    return centred * lax.rsqrt(spread + NORM_EPS) * norm_gain + norm_shift


def norm_back(values, norm_gain, norm_shift, row_grad):
    result, pull = jax.vjp(scaled_norm, values, norm_gain, norm_shift)
    return pull(row_grad)


def segment_of(seq_lens, row_total):
    seq_ends = jnp.cumsum(seq_lens)
    token_positions = jnp.arange(row_total, dtype=jnp.int32)
    return jnp.sum((token_positions[:, None] >= seq_ends[None, :]).astype(jnp.int32), axis=1)


def lane_gather(rows_low):
    return lax.all_gather(rows_low, "tensor", axis=0, tiled=True)


def lane_sum(term_fn, rows_here):
    return lax.psum_scatter(
        term_fn(jnp.int32(0), rows_here * lax.axis_size("tensor")).astype(jnp.bfloat16),
        "tensor",
        scatter_dimension=0,
        tiled=True,
    ).astype(jnp.float32)


def grad_gather(rows_low):
    return lax.all_gather(rows_low, "tensor", axis=0, tiled=True)


def grad_sum(term_fn, rows_here):
    return lax.psum_scatter(
        term_fn(jnp.int32(0), rows_here * lax.axis_size("tensor")).astype(jnp.bfloat16),
        "tensor",
        scatter_dimension=0,
        tiled=True,
    ).astype(jnp.float32)


def window_of(block_index, query_heads, key_pad, value_pad, segment, seg_pad):
    span = QBLK + MAXLEN
    first = block_index * QBLK
    query_block = lax.dynamic_slice_in_dim(query_heads, first, QBLK, 0)
    key_block = lax.dynamic_slice_in_dim(key_pad, first, span, 0)
    value_block = lax.dynamic_slice_in_dim(value_pad, first, span, 0)
    query_seg = lax.dynamic_slice_in_dim(segment, first, QBLK, 0)
    key_seg = lax.dynamic_slice_in_dim(seg_pad, first, span, 0)
    query_pos = first + jnp.arange(QBLK, dtype=jnp.int32)
    key_pos = first - MAXLEN + jnp.arange(span, dtype=jnp.int32)
    allowed = (key_pos[None, :] <= query_pos[:, None]) & (key_seg[None, :] == query_seg[:, None])
    return (query_block, key_block, value_block, allowed)


def block_scores(query_block, key_block, allowed):
    factor = 1.0 / (RELAX_FACTOR * math.sqrt(DH))
    raw_score = (
        jnp.einsum("qhd,khd->hqk", query_block, key_block, preferred_element_type=jnp.float32)
        * factor
    )
    return jnp.where(allowed[None], raw_score, MASKED_OUT)


def attn_forward(query_heads, key_pad, value_pad, segment, seg_pad):
    row_total = query_heads.shape[0]

    def one_block(block_index):
        query_block, key_block, value_block, allowed = window_of(
            block_index, query_heads, key_pad, value_pad, segment, seg_pad
        )
        masked = block_scores(query_block, key_block, allowed)
        row_peak = jnp.max(masked, axis=-1, keepdims=True)
        exponent = jnp.exp(RELAX_FACTOR * (masked - row_peak))
        row_totals = jnp.sum(exponent, axis=-1, keepdims=True)
        attn_prob = (exponent / row_totals).astype(jnp.bfloat16)
        mixed = jnp.einsum(
            "hqk,khd->qhd", attn_prob, value_block, preferred_element_type=jnp.float32
        )
        return (mixed.astype(jnp.bfloat16), row_peak, row_totals)

    mixed_all, peaks, sums_all = lax.map(one_block, jnp.arange(row_total // QBLK, dtype=jnp.int32))
    return (mixed_all.reshape(row_total, -1), peaks, sums_all)


def attn_backward(query_heads, key_pad, value_pad, segment, seg_pad, peaks, sums_all, grad_heads):
    row_total = query_heads.shape[0]
    span = QBLK + MAXLEN
    factor = 1.0 / (RELAX_FACTOR * math.sqrt(DH))
    start_grads = (jnp.zeros(key_pad.shape, jnp.float32), jnp.zeros(value_pad.shape, jnp.float32))

    def one_step(carry, block_index):
        key_grad, value_grad = carry
        first = block_index * QBLK
        query_block, key_block, value_block, allowed = window_of(
            block_index, query_heads, key_pad, value_pad, segment, seg_pad
        )
        grad_block = lax.dynamic_slice_in_dim(grad_heads, first, QBLK, 0)
        masked = block_scores(query_block, key_block, allowed)
        exponent = jnp.exp(RELAX_FACTOR * (masked - peaks[block_index]))
        attn_prob = exponent / sums_all[block_index]
        prob_low = attn_prob.astype(jnp.bfloat16)
        grad_prob = jnp.einsum(
            "qhd,khd->hqk", grad_block, value_block, preferred_element_type=jnp.float32
        )
        value_term = jnp.einsum(
            "hqk,qhd->khd", prob_low, grad_block, preferred_element_type=jnp.float32
        )
        inner = jnp.sum(grad_prob * attn_prob, axis=-1, keepdims=True)
        grad_score = jnp.where(
            allowed[None], RELAX_FACTOR * attn_prob * (grad_prob - inner), 0.0
        ).astype(jnp.bfloat16)
        query_term = (
            jnp.einsum("hqk,khd->qhd", grad_score, key_block, preferred_element_type=jnp.float32)
            * factor
        )
        key_term = (
            jnp.einsum("hqk,qhd->khd", grad_score, query_block, preferred_element_type=jnp.float32)
            * factor
        )
        key_grad = lax.dynamic_update_slice_in_dim(
            key_grad, lax.dynamic_slice_in_dim(key_grad, first, span, 0) + key_term, first, 0
        )
        value_grad = lax.dynamic_update_slice_in_dim(
            value_grad, lax.dynamic_slice_in_dim(value_grad, first, span, 0) + value_term, first, 0
        )
        return ((key_grad, value_grad), query_term)

    (key_grad, value_grad), query_terms = lax.scan(
        one_step, start_grads, jnp.arange(row_total // QBLK, dtype=jnp.int32)
    )
    query_grad = query_terms.reshape(row_total, -1)
    return (
        query_grad,
        key_grad[MAXLEN:].reshape(row_total, -1),
        value_grad[MAXLEN:].reshape(row_total, -1),
    )


def body(
    tokens, cotangent, lengths, deal, w_qkv, w_o, w_1, w_2, b_qv, b_o, b_1, b_2, ln_gain, ln_bias
):
    local_in, local_cot = (
        lax.all_to_all(tokens, "dp", split_axis=0, concat_axis=0, tiled=True),
        lax.all_to_all(cotangent, "dp", split_axis=0, concat_axis=0, tiled=True),
    )
    lane_count = lax.axis_size("tensor")
    group_index = lax.axis_index("dp")
    rows_here = local_in.shape[0]
    row_total = rows_here * lane_count
    seq_per = lengths.shape[0] // lax.axis_size("dp")
    picked = lax.dynamic_slice_in_dim(deal, group_index * seq_per, seq_per)
    lookup = picked[:, None] == jnp.arange(lengths.shape[0], dtype=jnp.int32)[None, :]
    seq_lens = jnp.sum(jnp.where(lookup, lengths[None, :], 0), axis=1)
    segment = segment_of(seq_lens, row_total)
    seg_pad = jnp.concatenate([jnp.full((MAXLEN,), -1, jnp.int32), segment])
    qkv_full, out_full = (
        lax.all_gather(w_qkv, "dp", axis=1, tiled=True),
        lax.all_gather(w_o, "dp", axis=1, tiled=True),
    )
    local_width = qkv_full.shape[2]
    head_count = local_width // DH
    hidden = local_in.astype(jnp.float32)
    normed_in = lane_gather(scaled_norm(hidden, ln_gain[0], ln_bias[0]).astype(jnp.bfloat16))
    projected = jnp.einsum("rd,sde->sre", normed_in, qkv_full, preferred_element_type=jnp.float32)
    query_rows = (projected[0] + b_qv[0]).astype(jnp.bfloat16)
    key_rows = projected[1].astype(jnp.bfloat16)
    value_rows = (projected[2] + b_qv[1]).astype(jnp.bfloat16)
    head_shape = (row_total, head_count, DH)
    pad_rows = jnp.zeros((MAXLEN, head_count, DH), jnp.bfloat16)
    query_heads = query_rows.reshape(head_shape)
    key_pad = jnp.concatenate([pad_rows, key_rows.reshape(head_shape)], 0)
    value_pad = jnp.concatenate([pad_rows, value_rows.reshape(head_shape)], 0)
    heads_out, peaks, sums_all = attn_forward(query_heads, key_pad, value_pad, segment, seg_pad)

    def out_term(first_row, row_count):
        return jnp.dot(heads_out, out_full, preferred_element_type=jnp.float32)

    attn_out = lane_sum(out_term, rows_here) + b_o
    first_sum = hidden + scaled_norm(attn_out, ln_gain[1], ln_bias[1])
    normed_mid = lane_gather(scaled_norm(first_sum, ln_gain[2], ln_bias[2]).astype(jnp.bfloat16))
    up_full, down_full = (
        lax.all_gather(w_1, "dp", axis=0, tiled=True),
        lax.all_gather(w_2, "dp", axis=1, tiled=True),
    )
    pre_act = jnp.dot(normed_mid, up_full, preferred_element_type=jnp.float32) + b_1
    act = jax.nn.gelu(pre_act, approximate=False).astype(jnp.bfloat16)

    def down_term(first_row, row_count):
        return jnp.dot(act, down_full, preferred_element_type=jnp.float32)

    feedforward_output = lane_sum(down_term, rows_here) + b_2
    result = first_sum + scaled_norm(feedforward_output, ln_gain[3], ln_bias[3])
    grad_result = local_cot.astype(jnp.float32)
    grad_ffn, gain_three, shift_three = norm_back(
        feedforward_output, ln_gain[3], ln_bias[3], grad_result
    )
    grad_ffn_low = grad_ffn.astype(jnp.bfloat16)
    bias_two_grad = jnp.sum(grad_ffn_low.astype(jnp.float32), axis=0)
    grad_ffn_full = grad_gather(grad_ffn_low)
    up_back, down_back = (
        lax.all_gather(w_1, "dp", axis=0, tiled=True),
        lax.all_gather(w_2, "dp", axis=1, tiled=True),
    )
    grad_act = jnp.einsum("rd,fd->rf", grad_ffn_full, down_back, preferred_element_type=jnp.float32)
    down_grad = jnp.einsum("rf,rd->fd", act, grad_ffn_full, preferred_element_type=jnp.float32)
    gelu_value, gelu_pull = jax.vjp(partial(jax.nn.gelu, approximate=False), pre_act)
    grad_pre = gelu_pull(grad_act)[0].astype(jnp.bfloat16)
    bias_one_grad = jnp.sum(grad_pre.astype(jnp.float32), axis=0)
    up_grad = jnp.einsum("rd,rf->df", normed_mid, grad_pre, preferred_element_type=jnp.float32)
    up_shard, down_shard = (up_grad, down_grad)

    def mid_term(first_row, row_count):
        return jnp.einsum("rf,df->rd", grad_pre, up_back, preferred_element_type=jnp.float32)

    grad_mid = grad_sum(mid_term, rows_here)
    grad_first_part, gain_two, shift_two = norm_back(first_sum, ln_gain[2], ln_bias[2], grad_mid)
    grad_first = grad_result + grad_first_part
    grad_attn, gain_one, shift_one = norm_back(attn_out, ln_gain[1], ln_bias[1], grad_first)
    grad_attn_low = grad_attn.astype(jnp.bfloat16)
    bias_out_grad = jnp.sum(grad_attn_low.astype(jnp.float32), axis=0)
    grad_attn_full = grad_gather(grad_attn_low)
    qkv_back, out_back = (
        lax.all_gather(w_qkv, "dp", axis=1, tiled=True),
        lax.all_gather(w_o, "dp", axis=1, tiled=True),
    )
    grad_heads = jnp.einsum(
        "rd,ed->re", grad_attn_full, out_back, preferred_element_type=jnp.float32
    ).astype(jnp.bfloat16)
    out_grad = jnp.einsum(
        "re,rd->ed", heads_out, grad_attn_full, preferred_element_type=jnp.float32
    )
    query_grad, key_grad, value_grad = attn_backward(
        query_heads,
        key_pad,
        value_pad,
        segment,
        seg_pad,
        peaks,
        sums_all,
        grad_heads.reshape(head_shape),
    )
    grad_qkv = jnp.stack([query_grad, key_grad, value_grad]).astype(jnp.bfloat16)
    grad_qkv_wide = grad_qkv.astype(jnp.float32)
    bias_qv_grad = jnp.stack([jnp.sum(grad_qkv_wide[0], axis=0), jnp.sum(grad_qkv_wide[2], axis=0)])
    qkv_grad = jnp.einsum("rd,sre->sde", normed_in, grad_qkv, preferred_element_type=jnp.float32)

    def input_term(first_row, row_count):
        return jnp.einsum("sre,sde->rd", grad_qkv, qkv_back, preferred_element_type=jnp.float32)

    grad_in = grad_sum(input_term, rows_here)
    grad_hidden_part, gain_zero, shift_zero = norm_back(hidden, ln_gain[0], ln_bias[0], grad_in)
    grad_hidden = grad_first + grad_hidden_part
    qkv_shard, out_shard, up_shard, down_shard = (
        lax.psum_scatter(qkv_grad, "dp", scatter_dimension=1, tiled=True),
        lax.psum_scatter(out_grad, "dp", scatter_dimension=1, tiled=True),
        lax.psum_scatter(up_grad, "dp", scatter_dimension=0, tiled=True),
        lax.psum_scatter(down_grad, "dp", scatter_dimension=1, tiled=True),
    )
    head_bias_qv, head_bias_one = lax.psum((bias_qv_grad, bias_one_grad), "dp")
    gain_stack = jnp.stack([gain_zero, gain_one, gain_two, gain_three])
    shift_stack = jnp.stack([shift_zero, shift_one, shift_two, shift_three])
    gain_total, offset_overall, bias_out_total, bias_two_total = lax.psum(
        (gain_stack, shift_stack, bias_out_grad, bias_two_grad), ("dp", "tensor")
    )
    output_rows, input_rows = (
        lax.all_to_all(result.astype(jnp.bfloat16), "dp", split_axis=0, concat_axis=0, tiled=True),
        lax.all_to_all(
            grad_hidden.astype(jnp.bfloat16), "dp", split_axis=0, concat_axis=0, tiled=True
        ),
    )
    return (
        output_rows,
        input_rows,
        qkv_shard,
        out_shard,
        up_shard,
        down_shard,
        head_bias_qv,
        bias_out_total,
        head_bias_one,
        bias_two_total,
        gain_total,
        offset_overall,
    )


def solution(mesh):
    placed = (
        P(("dp", "tensor"), None),
        P(("dp", "tensor"), None),
        P(),
        P(),
        P(None, "dp", "tensor"),
        P("tensor", "dp"),
        P("dp", "tensor"),
        P("tensor", "dp"),
        P(None, "tensor"),
        P(),
        P("tensor"),
        P(),
        P(),
        P(),
    )
    return jax.shard_map(
        body,
        mesh=mesh,
        in_specs=placed,
        out_specs=(
            P(("dp", "tensor"), None),
            P(("dp", "tensor"), None),
            P(None, "dp", "tensor"),
            P("tensor", "dp"),
            P("dp", "tensor"),
            P("tensor", "dp"),
            P(None, "tensor"),
            P(),
            P("tensor"),
            P(),
            P(),
            P(),
        ),
        check_vma=False,
    )
```

profile of v0, /device:TPU:0, one launch (start us, length us, event | category | flops | bytes accessed | tf_op | source)
XLA Modules:
  0.0 1348.8 jit_solution(9678845861428645542)
XLA Ops:
  14.7 13.3 all-to-all-done
  34.0 10.9 all_gather.30
  45.3 82.9 %all-gather.8.cloned.1.call-done = bf16[2048,1024]{1,0:T(8,128)(2,1)} async-done(((bf16[512,1024]{1,0:T(8,128)(2,1)}), bf16[2048,1024]{1,0:T(8,128)(2,1)}) %all-gather.8.cloned.1.call-update) | async-done | bytes 4194320 | tf_op jit(solution)/shard_map/all_gather | solution.py:36
  137.5 58.6 %while.32 = (s32[]{:T(128)}, bf16[4,512,4,64]{1,3,2,0:T(8,128)(2,1)}, f32[4,4,512,1]{2,1,3,0:T(4,128)S(1)}, f32[4,4,512,1]{2,1,3,0:T(4,128)S(1)}, s32[4]{0:T(128...) while((s32[]{:T(128)}, ...), condition=%wide.region_9.10_spmd, body=%wide.region_6.9_spmd.sunk | while | flops 851834880 | bytes 43106592 | solution.py:101
  204.2 74.6 %reduce-scatter.9.cloned.1.call-done = bf16[512,1024]{1,0:T(8,128)(2,1)} async-done(((bf16[2048,1024]{1,0:T(8,128)(2,1)}), bf16[512,1024]{1,0:T(8,128)(2,1)}) %reduce-scatter.9.cloned.1.call-update) | async-done | bytes 1048592 | tf_op jit(solution)/shard_map/reduce_scatter | solution.py:40
  286.5 22.6 %all-gather.14.cloned.1.call-done = bf16[1024,1024]{1,0:T(8,128)(2,1)} async-done(((bf16[128,1024]{1,0:T(8,128)(2,1)}), bf16[1024,1024]{1,0:T(8,128)(2,1)}) %all-gather.14.cloned.1.call-update) | async-done | bytes 2097168 | tf_op jit(solution)/shard_map/all_gather | solution.py:202
  309.1 82.9 %all-gather.12.cloned.1.call-done = bf16[2048,1024]{1,0:T(8,128)(2,1)} async-done(((bf16[512,1024]{1,0:T(8,128)(2,1)}), bf16[2048,1024]{1,0:T(8,128)(2,1)}) %all-gather.12.cloned.1.call-update) | async-done | bytes 4194320 | tf_op jit(solution)/shard_map/all_gather | solution.py:36
  392.0 26.2 %multiply_convert_fusion = (bf16[2048,1024]{1,0:T(8,128)(2,1)}, f32[2048,1024]{1,0:T(8,128)}, f32[2048,1024]{1,0:T(8,128)}) fusion(f32[1024]{0:T(1024)S(1)} %copy-done.58, bf16[2048,1024]{1,0:T(8,128)(2,1)} %all-gather.12.cloned.1.call-done, bf16[1024,1024]{1,0:T(8,128)(2,1)} %all-gather.14.cloned.1.call-done), kind=kOutput, calls=%fused_computation.69 | convolution fusion | flops 4433379328 | bytes 27267072 | tf_op jit(solution)/shard_map/dot_general | solution.py:205
  420.6 9.3 convolution_convert_fusion.2
  434.7 72.2 %reduce-scatter.11.cloned.1.call-done = bf16[512,1024]{1,0:T(8,128)(2,1)} async-done(((bf16[2048,1024]{1,0:T(8,128)(2,1)}), bf16[512,1024]{1,0:T(8,128)(2,1)}) %reduce-scatter.11.cloned.1.call-update) | async-done | bytes 1048592 | tf_op jit(solution)/shard_map/reduce_scatter | solution.py:40
  519.4 81.4 %all-gather.18.cloned.1.call-done = bf16[2048,1024]{1,0:T(8,128)(2,1)} async-done(((bf16[512,1024]{1,0:T(8,128)(2,1)}), bf16[2048,1024]{1,0:T(8,128)(2,1)}) %all-gather.18.cloned.1.call-update) | async-done | bytes 4194320 | tf_op jit(solution)/shard_map/all_gather | solution.py:49
  600.8 14.0 %convert_reduce_fusion = (f32[1024]{0:T(1024)}, bf16[2048,1024]{1,0:T(8,128)(2,1)S(1)}) fusion(f32[2048,1024]{1,0:T(8,128)} %get-tuple-element.431, f32[2048,1024]{1,0:T(8,128)} %get-tuple-element.460, f32[1024]{0:T(1024)S(1)} %copy-done.58, bf16[2048,1024]{1,0:T(8,128)(2,1)} %all-gather.18.cloned.1.call-done, ...), kind=kOutput, calls=%fused_computation.67 | convolution fusion | flops 4330617856 | bytes 27271168 | tf_op jit(solution)/shard_map/rd,fd->rf/dot_general | solution.py:224
  623.3 75.2 %reduce-scatter.13.cloned.1.call-done = bf16[512,1024]{1,0:T(8,128)(2,1)} async-done(((bf16[2048,1024]{1,0:T(8,128)(2,1)}), bf16[512,1024]{1,0:T(8,128)(2,1)}) %reduce-scatter.13.cloned.1.call-update) | async-done | bytes 1048592 | tf_op jit(solution)/shard_map/reduce_scatter | solution.py:53
  713.9 81.4 %all-gather.20.cloned.1.call-done = bf16[2048,1024]{1,0:T(8,128)(2,1)} async-done(((bf16[512,1024]{1,0:T(8,128)(2,1)}), bf16[2048,1024]{1,0:T(8,128)(2,1)}) %all-gather.20.cloned.1.call-update) | async-done | bytes 4194320 | tf_op jit(solution)/shard_map/all_gather | solution.py:49
  803.7 238.9 %while.33 = (s32[]{:T(128)}, f32[3072,4,64]{0,2,1:T(8,128)}, f32[3072,4,64]{0,2,1:T(8,128)}, bf16[4,512,4,64]{1,3,2,0:T(8,128)(2,1)}, s32[4]{0:T(128)S(1)}, /*in...) while((s32[]{:T(128)}, f32[3072,4,64]{0,2,1:T(8,128)}, ...), condition=%wide.region_36.37_spmd, body=%wide.region_34.36_spmd.sunk | while | flops 2073568256 | bytes 206397872 | solution.py:148
  824.9 18.0 %fusion.211 = bf16[4,512,4,64]{1,3,2,0:T(8,128)(2,1)} fusion(bf16[4,512,4,64]{1,3,2,0:T(8,128)(2,1)} %get-tuple-element.686, s32[]{:T(128)S(6)} %copy.78, f32[4,512,1536]{2,1,0:T(8,128)} %fusion.208, f32[4,512,1536]{2,1,0:T(8,128)} %copy-done, pred[512,1536]{1,0:T(8,128)(4,1)S(1)} %compare_and_fusion.5, ...), kind=kOutput, calls=%fused_computation.42.clone.1 | convolution fusion | flops 421662208 | bytes 52428808 | tf_op jit(solution)/shard_map/while/body/eval_jaxpr/hqk,khd->qhd/dot_general | solution.py:133
  842.9 20.6 %fusion.209 = f32[3072,4,64]{0,2,1:T(8,128)} fusion(f32[3072,4,64]{0,2,1:T(8,128)} %get-tuple-element.684, s32[]{:T(128)S(6)} %select_n.214, f32[4,512,1536]{2,1,0:T(8,128)} %fusion.208, f32[4,512,1536]{2,1,0:T(8,128)} %copy-done, pred[512,1536]{1,0:T(8,128)(4,1)S(1)} %compare_and_fusion.5, bf16[2048,4,64]{0,2,1:T(8,128)(2,1)} %get-tuple-element.708, ...), kind=kOutput, calls=%fused_computation.36.clone.1 | convolution fusion | flops 422317568 | bytes 54525960 | tf_op jit(solution)/shard_map/while/body/eval_jaxpr/hqk,qhd->khd/dot_general | solution.py:137
  884.5 18.1 %fusion.211 = bf16[4,512,4,64]{1,3,2,0:T(8,128)(2,1)} fusion(bf16[4,512,4,64]{1,3,2,0:T(8,128)(2,1)} %get-tuple-element.686, s32[]{:T(128)S(6)} %copy.78, f32[4,512,1536]{2,1,0:T(8,128)} %fusion.208, f32[4,512,1536]{2,1,0:T(8,128)} %copy-done, pred[512,1536]{1,0:T(8,128)(4,1)S(1)} %compare_and_fusion.5, ...), kind=kOutput, calls=%fused_computation.42.clone.1 | convolution fusion | flops 421662208 | bytes 52428808 | tf_op jit(solution)/shard_map/while/body/eval_jaxpr/hqk,khd->qhd/dot_general | solution.py:133
  902.6 20.5 %fusion.209 = f32[3072,4,64]{0,2,1:T(8,128)} fusion(f32[3072,4,64]{0,2,1:T(8,128)} %get-tuple-element.684, s32[]{:T(128)S(6)} %select_n.214, f32[4,512,1536]{2,1,0:T(8,128)} %fusion.208, f32[4,512,1536]{2,1,0:T(8,128)} %copy-done, pred[512,1536]{1,0:T(8,128)(4,1)S(1)} %compare_and_fusion.5, bf16[2048,4,64]{0,2,1:T(8,128)(2,1)} %get-tuple-element.708, ...), kind=kOutput, calls=%fused_computation.36.clone.1 | convolution fusion | flops 422317568 | bytes 54525960 | tf_op jit(solution)/shard_map/while/body/eval_jaxpr/hqk,qhd->khd/dot_general | solution.py:137
  944.1 18.1 %fusion.211 = bf16[4,512,4,64]{1,3,2,0:T(8,128)(2,1)} fusion(bf16[4,512,4,64]{1,3,2,0:T(8,128)(2,1)} %get-tuple-element.686, s32[]{:T(128)S(6)} %copy.78, f32[4,512,1536]{2,1,0:T(8,128)} %fusion.208, f32[4,512,1536]{2,1,0:T(8,128)} %copy-done, pred[512,1536]{1,0:T(8,128)(4,1)S(1)} %compare_and_fusion.5, ...), kind=kOutput, calls=%fused_computation.42.clone.1 | convolution fusion | flops 421662208 | bytes 52428808 | tf_op jit(solution)/shard_map/while/body/eval_jaxpr/hqk,khd->qhd/dot_general | solution.py:133
  962.2 20.5 %fusion.209 = f32[3072,4,64]{0,2,1:T(8,128)} fusion(f32[3072,4,64]{0,2,1:T(8,128)} %get-tuple-element.684, s32[]{:T(128)S(6)} %select_n.214, f32[4,512,1536]{2,1,0:T(8,128)} %fusion.208, f32[4,512,1536]{2,1,0:T(8,128)} %copy-done, pred[512,1536]{1,0:T(8,128)(4,1)S(1)} %compare_and_fusion.5, bf16[2048,4,64]{0,2,1:T(8,128)(2,1)} %get-tuple-element.708, ...), kind=kOutput, calls=%fused_computation.36.clone.1 | convolution fusion | flops 422317568 | bytes 54525960 | tf_op jit(solution)/shard_map/while/body/eval_jaxpr/hqk,qhd->khd/dot_general | solution.py:137
  1003.6 18.1 %fusion.211 = bf16[4,512,4,64]{1,3,2,0:T(8,128)(2,1)} fusion(bf16[4,512,4,64]{1,3,2,0:T(8,128)(2,1)} %get-tuple-element.686, s32[]{:T(128)S(6)} %copy.78, f32[4,512,1536]{2,1,0:T(8,128)} %fusion.208, f32[4,512,1536]{2,1,0:T(8,128)} %copy-done, pred[512,1536]{1,0:T(8,128)(4,1)S(1)} %compare_and_fusion.5, ...), kind=kOutput, calls=%fused_computation.42.clone.1 | convolution fusion | flops 421662208 | bytes 52428808 | tf_op jit(solution)/shard_map/while/body/eval_jaxpr/hqk,khd->qhd/dot_general | solution.py:133
  1021.7 20.4 %fusion.209 = f32[3072,4,64]{0,2,1:T(8,128)} fusion(f32[3072,4,64]{0,2,1:T(8,128)} %get-tuple-element.684, s32[]{:T(128)S(6)} %select_n.214, f32[4,512,1536]{2,1,0:T(8,128)} %fusion.208, f32[4,512,1536]{2,1,0:T(8,128)} %copy-done, pred[512,1536]{1,0:T(8,128)(4,1)S(1)} %compare_and_fusion.5, bf16[2048,4,64]{0,2,1:T(8,128)(2,1)} %get-tuple-element.708, ...), kind=kOutput, calls=%fused_computation.36.clone.1 | convolution fusion | flops 422317568 | bytes 54525960 | tf_op jit(solution)/shard_map/while/body/eval_jaxpr/hqk,qhd->khd/dot_general | solution.py:137
  1068.0 10.0 fusion.154
  1078.3 10.0 fusion.155
  1098.0 37.9 %reduce-scatter.15.cloned.1.call-done = bf16[512,1024]{1,0:T(8,128)(2,1)} async-done(((bf16[2048,1024]{1,0:T(8,128)(2,1)}), bf16[512,1024]{1,0:T(8,128)(2,1)}) %reduce-scatter.15.cloned.1.call-update) | async-done | bytes 1048592 | tf_op jit(solution)/shard_map/reduce_scatter | solution.py:53
  1150.5 20.3 %all-reduce.4 = (f32[2,256]{1,0:T(2,128)}, f32[1024]{0:T(1024)}) all-reduce(f32[2,256]{1,0:T(2,128)S(1)} %pad_maximum_fusion.3, f32[1024]{0:T(1024)S(1)} %copy-done.55), channel_id=1, replica_groups=mesh['dp'=8,'tensor'=4] {'dp'}, use_global_device_ids=true, to_apply=%region_48.49 | all-reduce | flops 1536 | bytes 12288 | tf_op jit(solution)/shard_map/psum | solution.py:279
  1170.9 15.4 %reduce-scatter.17.cloned.1.call-done = f32[3,128,256]{1,2,0:T(8,128)} async-done(((f32[3,1024,256]{1,2,0:T(8,128)}), f32[3,128,256]{1,2,0:T(8,128)}) %reduce-scatter.17.cloned.1.call-update) | async-done | bytes 393232 | tf_op jit(solution)/shard_map/reduce_scatter | solution.py:274
  1188.3 40.5 %all-reduce.3 = (f32[1024]{0:T(1024)}, f32[1024]{0:T(1024)}, f32[4,1024]{1,0:T(4,128)}, f32[4,1024]{1,0:T(4,128)}) all-reduce(f32[1024]{0:T(1024)S(1)} %copy-done.53, f32[1024]{0:T(1024)S(1)} %copy-done.52, f32[4,1024]{1,0:T(4,128)S(1)} %get-tuple-element.461, ...), channel_id=1, replica_groups=mesh['dp'=8,'tensor'=4] {'dp','tensor'}, use_global_device_ids=true, to_apply=%region_50.51 | all-reduce | flops 10240 | bytes 81920 | tf_op jit(solution)/shard_map/psum | solution.py:282
  1228.8 13.6 %reduce-scatter.21.cloned.1.call-done = f32[128,1024]{1,0:T(8,128)} async-done(((f32[1024,1024]{1,0:T(8,128)}), f32[128,1024]{1,0:T(8,128)}) %reduce-scatter.21.cloned.1.call-update) | async-done | bytes 524304 | tf_op jit(solution)/shard_map/reduce_scatter | solution.py:276
  1242.4 55.1 %reduce-scatter.23.cloned.1.call-done = f32[1024,128]{1,0:T(8,128)} async-done(((f32[1024,1024]{1,0:T(8,128)}), f32[1024,128]{1,0:T(8,128)}) %reduce-scatter.23.cloned.1.call-update) | async-done | bytes 524304 | tf_op jit(solution)/shard_map/reduce_scatter | solution.py:277
  1297.5 40.0 %reduce-scatter.19.cloned.1.call-done = f32[256,128]{1,0:T(8,128)} async-done(((f32[256,1024]{1,0:T(8,128)}), f32[256,128]{1,0:T(8,128)}) %reduce-scatter.19.cloned.1.call-update) | async-done | bytes 131088 | tf_op jit(solution)/shard_map/reduce_scatter | solution.py:275
  (362 shorter events, 275.9 us)
Async XLA Ops:
  7.2 20.7 %all-to-all-start = ((bf16[8,64,1024]{2,1,0:T(8,128)(2,1)}), bf16[8,64,1024]{2,1,0:T(8,128)(2,1)S(1)}, u32[]{:S(2)}, u32[]{:S(2)}) async-start(bf16[8,64,1024]{2,1,0:T(8,128)(2,1)} %bitcast.177), calls=%async_computation | async-start | bytes 2097152 | tf_op jit(solution)/shard_map/all_to_all | solution.py:163
  12.5 32.8 %all-gather.10.cloned.1.call-start = ((), (), s32[]{:S(2)}) async-start(), calls=%async_computation.13 | async-start | bytes 1769472 | tf_op jit(solution)/shard_map/all_gather | solution.py:177
  13.4 114.9 %all-gather.8.cloned.1.call-start = ((), (), s32[]{:S(2)}) async-start(), calls=%async_computation.12 | async-start | bytes 5242880 | tf_op jit(solution)/shard_map/all_gather | solution.py:36
  28.0 254.6 %copy-start.1 = (bf16[8,64,1024]{2,1,0:T(8,128)(2,1)}, bf16[8,64,1024]{2,1,0:T(8,128)(2,1)S(1)}, u32[]{:S(2)}) copy-start(bf16[8,64,1024]{2,1,0:T(8,128)(2,1)S(1)} %all-to-all-done) | copy-start | bytes 3145732
  30.3 103.7 %copy-start.39 = (f32[512]{0:T(512)}, f32[512]{0:T(512)S(1)}, u32[]{:S(2)}) copy-start(f32[512]{0:T(512)S(1)} %add.362) | copy-start | bytes 6148
  30.4 103.7 %copy-start.35 = (f32[512]{0:T(512)}, f32[512]{0:T(512)S(1)}, u32[]{:S(2)}) copy-start(f32[512]{0:T(512)S(1)} %rsqrt.44) | copy-start | bytes 6148
  33.1 245.6 %reduce-scatter.9.cloned.1.call-start = ((), (), s32[]{:S(2)}) async-start(), calls=%async_computation.14 | async-start | bytes 5242880 | tf_op jit(solution)/shard_map/reduce_scatter | solution.py:40
  44.8 154.3 %copy-start.20 = (bf16[256,1024]{1,0:T(8,128)(2,1)}, bf16[256,1024]{1,0:T(8,128)(2,1)S(1)}, u32[]{:S(2)}) copy-start(bf16[256,1024]{1,0:T(8,128)(2,1)S(1)} %all_gather.30) | copy-start | bytes 1572868
  203.3 75.5 %copy-start.22 = (f32[1024]{0:T(1024)S(1)}, f32[1024]{0:T(1024)}, u32[]{:S(2)}) copy-start(f32[1024]{0:T(1024)} %param.27) | copy-start | bytes 12292
  203.3 79.3 %copy-start.31 = (f32[1,1024]{1,0:T(1,128)S(1)}, f32[1,1024]{1,0:T(1,128)}, u32[]{:S(2)}) copy-start(f32[1,1024]{1,0:T(1,128)} %get-tuple-element.445) | copy-start | bytes 12292
  203.3 79.3 %copy-start.49 = (f32[1,1024]{1,0:T(1,128)S(1)}, f32[1,1024]{1,0:T(1,128)}, u32[]{:S(2)}) copy-start(f32[1,1024]{1,0:T(1,128)} %get-tuple-element.449) | copy-start | bytes 12292
  203.3 105.8 %all-gather.14.cloned.1.call-start = ((), (), s32[]{:S(2)}) async-start(), calls=%async_computation.16 | async-start | bytes 2359296 | tf_op jit(solution)/shard_map/all_gather | solution.py:202
  203.9 188.0 %all-gather.12.cloned.1.call-start = ((), (), s32[]{:S(2)}) async-start(), calls=%async_computation.15 | async-start | bytes 5242880 | tf_op jit(solution)/shard_map/all_gather | solution.py:36
  284.4 107.6 %copy-start.58 = (f32[1024]{0:T(1024)S(1)}, f32[1024]{0:T(1024)}, u32[]{:S(2)}) copy-start(f32[1024]{0:T(1024)} %param.28) | copy-start | bytes 12292
  285.9 134.7 %all-gather.16.cloned.1.call-start = ((), (), s32[]{:S(2)}) async-start(), calls=%async_computation.17 | async-start | bytes 2359296 | tf_op jit(solution)/shard_map/all_gather | solution.py:203
  286.4 220.4 %reduce-scatter.11.cloned.1.call-start = ((), (), s32[]{:S(2)}) async-start(), calls=%async_computation.18 | async-start | bytes 5242880 | tf_op jit(solution)/shard_map/reduce_scatter | solution.py:40
  429.9 76.9 %copy-start.23 = (f32[1024]{0:T(1024)S(1)}, f32[1024]{0:T(1024)}, u32[]{:S(2)}) copy-start(f32[1024]{0:T(1024)} %param.29) | copy-start | bytes 12292
  430.0 80.7 %all-to-all-start.2 = ((bf16[8,64,1024]{2,1,0:T(8,128)(2,1)}), bf16[8,64,1024]{2,1,0:T(8,128)(2,1)}, u32[]{:S(2)}, u32[]{:S(2)}) async-start(bf16[8,64,1024]{2,1,0:T(8,128)(2,1)} %bitcast.31), calls=%async_computation.4 | async-start | bytes 2097152 | tf_op jit(solution)/shard_map/all_to_all | solution.py:164
  434.2 76.5 %copy-start.33 = (f32[1,1024]{1,0:T(1,128)S(1)}, f32[1,1024]{1,0:T(1,128)}, u32[]{:S(2)}) copy-start(f32[1,1024]{1,0:T(1,128)} %get-tuple-element.447) | copy-start | bytes 12292
  434.2 166.6 %all-gather.18.cloned.1.call-start = ((), (), s32[]{:S(2)}) async-start(), calls=%async_computation.19 | async-start | bytes 5242880 | tf_op jit(solution)/shard_map/all_gather | solution.py:49
  519.4 179.2 %reduce-scatter.13.cloned.1.call-start = ((), (), s32[]{:S(2)}) async-start(), calls=%async_computation.20 | async-start | bytes 5242880 | tf_op jit(solution)/shard_map/reduce_scatter | solution.py:53
  623.1 172.1 %all-gather.20.cloned.1.call-start = ((), (), s32[]{:S(2)}) async-start(), calls=%async_computation.21 | async-start | bytes 5242880 | tf_op jit(solution)/shard_map/all_gather | solution.py:49
  711.2 84.1 %copy-start.21 = (bf16[256,1024]{1,0:T(8,128)(2,1)S(1)}, bf16[256,1024]{1,0:T(8,128)(2,1)}, u32[]{:S(2)}) copy-start(bf16[256,1024]{1,0:T(8,128)(2,1)} %copy-done.20) | copy-start | bytes 1572868
  713.8 422.1 %reduce-scatter.15.cloned.1.call-start = ((), (), s32[]{:S(2)}) async-start(), calls=%async_computation.22 | async-start | bytes 5242880 | tf_op jit(solution)/shard_map/reduce_scatter | solution.py:53
  1060.5 125.8 %reduce-scatter.17.cloned.1.call-start = ((), (), s32[]{:S(2)}) async-start(), calls=%async_computation.23 | async-start | bytes 3538944 | tf_op jit(solution)/shard_map/reduce_scatter | solution.py:274
  1068.0 174.4 %reduce-scatter.21.cloned.1.call-start = ((), (), s32[]{:S(2)}) async-start(), calls=%async_computation.25 | async-start | bytes 4718592 | tf_op jit(solution)/shard_map/reduce_scatter | solution.py:276
  1078.0 219.5 %reduce-scatter.23.cloned.1.call-start = ((), (), s32[]{:S(2)}) async-start(), calls=%async_computation.26 | async-start | bytes 4718592 | tf_op jit(solution)/shard_map/reduce_scatter | solution.py:277
  1089.0 54.4 %all-to-all-start.1 = ((bf16[8,64,1024]{2,1,0:T(8,128)(2,1)}), bf16[8,64,1024]{2,1,0:T(8,128)(2,1)}, u32[]{:S(2)}, u32[]{:S(2)}) async-start(bf16[8,64,1024]{2,1,0:T(8,128)(2,1)} %bitcast.29), calls=%async_computation.3 | async-start | bytes 2097152 | tf_op jit(solution)/shard_map/all_to_all | solution.py:286
  1093.3 42.6 %copy-start.2 = (bf16[8,64,1024]{2,1,0:T(8,128)(2,1)S(1)}, bf16[8,64,1024]{2,1,0:T(8,128)(2,1)}, u32[]{:S(2)}) copy-start(bf16[8,64,1024]{2,1,0:T(8,128)(2,1)} %copy-done.1) | copy-start | bytes 3145732
  1093.3 42.6 %copy-start.26 = (f32[1,1024]{1,0:T(1,128)S(1)}, f32[1,1024]{1,0:T(1,128)}, u32[]{:S(2)}) copy-start(f32[1,1024]{1,0:T(1,128)} %copy-done.25) | copy-start | bytes 12292
  1093.3 244.2 %reduce-scatter.19.cloned.1.call-start = ((), (), s32[]{:S(2)}) async-start(), calls=%async_computation.24 | async-start | bytes 1179648 | tf_op jit(solution)/shard_map/reduce_scatter | solution.py:275
  1143.4 85.4 %all-to-all-start.3 = ((bf16[8,64,1024]{2,1,0:T(8,128)(2,1)}), bf16[8,64,1024]{2,1,0:T(8,128)(2,1)}, u32[]{:S(2)}, u32[]{:S(2)}) async-start(bf16[8,64,1024]{2,1,0:T(8,128)(2,1)} %bitcast.172), calls=%async_computation.7 | async-start | bytes 2097152 | tf_op jit(solution)/shard_map/all_to_all | solution.py:287
  (55 other events, 670.8 us)
Sparse Core Ops, SparseCore 0:
  15.8 29.4 all-gather.9
  47.5 80.7 all-gather.7
  203.4 75.2 reduce-scatter.8
  280.6 28.4 all-gather.13
  311.2 80.7 all-gather.11
  393.8 26.7 all-gather.15
  430.1 76.7 reduce-scatter.10
  519.5 81.2 all-gather.17
  623.2 75.2 reduce-scatter.12
  713.9 81.2 all-gather.19
  1060.6 75.2 reduce-scatter.14
  1139.2 47.0 reduce-scatter.16
  1190.6 51.7 reduce-scatter.20
  1246.1 51.3 reduce-scatter.22
  1301.4 36.0 reduce-scatter.18
where the time goes:
time: 1350 us
  waiting for transfers between devices  753 us (56%)
  matrix products  364 us (27%)
  blocking collectives  71.8 us (5%)
  other arithmetic  71 us (5%)
  local copies, waits for them, and re-layouts  40.9 us (3%)
  starting transfers between devices  19.8 us (1%)
  between operations  15 us (1%)
  loops' own time  13.9 us (1%)
    all_gather x2, waiting for transfers between devices, lane_gather(): return lax.all_gather(rows_low, 'tensor', axis=0, tiled=True)  166 us
    all_gather x2, waiting for transfers between devices, grad_gather(): return lax.all_gather(rows_low, 'tensor', axis=0, tiled=True)  163 us
    reduce_scatter x2, waiting for transfers between devices, lane_sum(): lax.psum_scatter(term_fn(jnp.int32(0), rows_here * lax.axis_size('tensor'...  147 us
    reduce_scatter x2, waiting for transfers between devices, grad_sum(): lax.psum_scatter(term_fn(jnp.int32(0), rows_here * lax.axis_size('tensor'...  113 us
    dot_general x4, matrix products, one_step(): jnp.einsum('hqk,qhd->khd', grad_score, query_block, preferred_element_typ...  82 us
    dot_general x4, matrix products, one_step(): jnp.einsum('hqk,khd->qhd', grad_score, key_block, preferred_element_type=...  72.3 us
    reduce_scatter x1, waiting for transfers between devices, body(): lax.psum_scatter(down_grad, 'dp', scatter_dimension=1, tiled=True)  55.1 us
    psum x1, blocking collectives, body(): lax.psum((gain_stack, shift_stack, bias_out_grad, bias_two_grad), ('dp',...  40.5 us
  transfers between devices with their start and end apart: 19, of which 16 were waited for; matrix products, arithmetic and copies ran while one was open for 7% of the time, Pallas kernels for 0%

commit v1 on v0

--- a/solution.py
+++ b/solution.py
@@ -13,6 +13,18 @@
 MASKED_OUT = -1000000000.0
 
 
+def collect(x, axis, dim):
+    ways, here = (lax.axis_size(axis), lax.axis_index(axis))
+    grown, reach = (x, 1)
+    while reach < ways:
+        theirs = lax.ppermute(grown, axis, [(d, d ^ reach) for d in range(ways)])
+        mine_first = jnp.concatenate([grown, theirs], axis=dim)
+        theirs_first = jnp.concatenate([theirs, grown], axis=dim)
+        grown = jnp.where(here & reach == 0, mine_first, theirs_first)
+        reach = 2 * reach
+    return grown
+
+
 def scaled_norm(values, norm_gain, norm_shift):
     peak = jnp.max(jnp.abs(values), axis=-1, keepdims=True) + NORM_EPS
     scaled = values / peak
@@ -33,7 +45,7 @@
 
 
 def lane_gather(rows_low):
-    return lax.all_gather(rows_low, "tensor", axis=0, tiled=True)
+    return collect(rows_low, "tensor", 0)
 
 
 def lane_sum(term_fn, rows_here):

time: 1350 us -> 1400 us (1.037)
  matrix products: 364 us -> 343 us
  local copies, waits for them, and re-layouts: 40.9 us -> 60.5 us
  waiting for transfers between devices: 753 us -> 772 us
    ppermute x0 -> x4, waiting for transfers between devices: none -> 206 us  [collect(): theirs = lax.ppermute(grown, axis, [(d, d ^ reach) for d in range(ways)])]
    all_gather x2 -> x0, waiting for transfers between devices: 166 us -> none  [lane_gather(): return lax.all_gather(rows_low, 'tensor', axis=0, tiled=True)]
    reduce_scatter x1, waiting for transfers between devices: 13.6 us -> 55.1 us  [body(): lax.psum_scatter(up_grad, 'dp', scatter_dimension=0, tiled=True)]
    reduce_scatter x1, waiting for transfers between devices: 55.1 us -> 13.6 us  [body(): lax.psum_scatter(down_grad, 'dp', scatter_dimension=1, tiled=True)]
    all_gather x1, waiting for transfers between devices: 22.6 us -> 0.02 us  [body(): lax.all_gather(w_1, 'dp', axis=0, tiled=True)]
    while x16 -> x32, local copies, waits for them, and re-layouts: 0.47 us -> 16.8 us
    dot_general x4, matrix products: 20.4 us -> 5.61 us  [one_step(): jnp.einsum('hqk,qhd->khd', prob_low, grad_block, preferred_element_type=j...]
  transfers between devices with their start and end apart: 19 -> 21, of which waited for: 16 -> 15; matrix products, arithmetic and copies ran while one was open for 7% -> 7% of each run, Pallas kernels for 0% -> 0%
where the time goes in v1:
time: 1400 us; the launch traced here: 1390 us
  waiting for transfers between devices  772 us (55%)
  matrix products  343 us (24%)
  other arithmetic  82.4 us (6%)
  blocking collectives  73.9 us (5%)
  local copies, waits for them, and re-layouts  60.5 us (4%)
  starting transfers between devices  28.4 us (2%)
  between operations  14.9 us (1%)
    ppermute x4, waiting for transfers between devices, collect(): theirs = lax.ppermute(grown, axis, [(d, d ^ reach) for d in range(ways)])  206 us
    all_gather x2, waiting for transfers between devices, grad_gather(): return lax.all_gather(rows_low, 'tensor', axis=0, tiled=True)  163 us
    reduce_scatter x2, waiting for transfers between devices, lane_sum(): lax.psum_scatter(term_fn(jnp.int32(0), rows_here * lax.axis_size('tensor'...  154 us
    reduce_scatter x2, waiting for transfers between devices, grad_sum(): lax.psum_scatter(term_fn(jnp.int32(0), rows_here * lax.axis_size('tensor'...  110 us
    dot_general x4, matrix products, one_step(): jnp.einsum('hqk,qhd->khd', grad_score, query_block, preferred_element_typ...  77 us
    dot_general x4, matrix products, one_step(): jnp.einsum('hqk,khd->qhd', grad_score, key_block, preferred_element_type=...  73.3 us
    reduce_scatter x1, waiting for transfers between devices, body(): lax.psum_scatter(up_grad, 'dp', scatter_dimension=0, tiled=True)  55.1 us
    psum x1, blocking collectives, body(): lax.psum((gain_stack, shift_stack, bias_out_grad, bias_two_grad), ('dp',...  40.5 us
  transfers between devices with their start and end apart: 21, of which 15 were waited for; matrix products, arithmetic and copies ran while one was open for 7% of the time, Pallas kernels for 0%

profile of v1, /device:TPU:0, one launch (start us, length us, event | category | flops | bytes accessed | tf_op | source)
XLA Modules:
  0.0 1389.4 jit_solution(10514000678118401020)
XLA Ops:
  13.8 14.1 %all-to-all-done = bf16[8,64,1024]{2,1,0:T(8,128)(2,1)S(1)} async-done(((bf16[8,64,1024]{2,1,0:T(8,128)(2,1)}), bf16[8,64,1024]{2,1,0:T(8,128)(2,1)S(1)}, u32[]{:S(2)}, u32[]{:S(2)}) %all-to-all-start) | async-done | bytes 1048608 | tf_op jit(solution)/shard_map/all_to_all | solution.py:175
  35.2 19.6 %collective-permute-done = bf16[512,1024]{1,0:T(8,128)(2,1)S(1)} collective-permute-done((bf16[512,1024]{1,0:T(8,128)(2,1)S(1)}, bf16[512,1024]{1,0:T(8,128)(2,1)S(1)}, u32[]{:S(2)}, u32[]{:S(2)}) %collective-permute-start) | collective-permute-done | bytes 1048608 | tf_op jit(solution)/shard_map/ppermute | solution.py:20
  60.5 13.0 all_gather.23
  73.5 73.4 %collective-permute-done.1 = bf16[1024,1024]{1,0:T(8,128)(2,1)S(1)} collective-permute-done((bf16[1024,1024]{1,0:T(8,128)(2,1)}, bf16[1024,1024]{1,0:T(8,128)(2,1)S(1)}, u32[]{:S(2)}, u32[]{:S(2)}) %collective-permute-start.1) | collective-permute-done | bytes 2097184 | tf_op jit(solution)/shard_map/ppermute | solution.py:20
  155.9 57.8 %while.32 = (s32[]{:T(128)}, bf16[4,512,4,64]{1,3,2,0:T(8,128)(2,1)}, f32[4,4,512,1]{2,1,3,0:T(4,128)S(1)}, f32[4,4,512,1]{2,1,3,0:T(4,128)S(1)}, s32[4]{0:T(128...) while((s32[]{:T(128)}, ...), condition=%wide.region_9.10_spmd, body=%wide.region_6.9_spmd.sunk | while | flops 851834880 | bytes 43106592 | solution.py:113
  222.1 81.3 %reduce-scatter.9.cloned.1.call-done = bf16[512,1024]{1,0:T(8,128)(2,1)} async-done(((bf16[2048,1024]{1,0:T(8,128)(2,1)}), bf16[512,1024]{1,0:T(8,128)(2,1)}) %reduce-scatter.9.cloned.1.call-update) | async-done | bytes 1048592 | tf_op jit(solution)/shard_map/reduce_scatter | solution.py:52
  311.1 23.4 %collective-permute-done.2 = bf16[512,1024]{1,0:T(8,128)(2,1)S(1)} collective-permute-done((bf16[512,1024]{1,0:T(8,128)(2,1)S(1)}, bf16[512,1024]{1,0:T(8,128)(2,1)S(1)}, u32[]{:S(2)}, u32[]{:S(2)}) %collective-permute-start.2) | collective-permute-done | bytes 1048608 | tf_op jit(solution)/shard_map/ppermute | solution.py:20
  340.0 90.0 %collective-permute-done.3 = bf16[1024,1024]{1,0:T(8,128)(2,1)} collective-permute-done((bf16[1024,1024]{1,0:T(8,128)(2,1)}, bf16[1024,1024]{1,0:T(8,128)(2,1)}, u32[]{:S(2)}, u32[]{:S(2)}) %collective-permute-start.3) | collective-permute-done | bytes 2097184 | tf_op jit(solution)/shard_map/ppermute | solution.py:20
  429.9 28.0 %multiply_convert_fusion = (bf16[2048,1024]{1,0:T(8,128)(2,1)}, f32[2048,1024]{1,0:T(8,128)}, f32[2048,1024]{1,0:T(8,128)}) fusion(f32[1024]{0:T(1024)S(1)} %copy-done.60, bf16[1024,1024]{1,0:T(8,128)(2,1)} %all-gather.8.cloned.1.call-done, bf16[1024,1024]{1,0:T(8,128)(2,1)} %collective-permute-done.3, bf16[1024,1024]{1,0:T(8,128)(2,1)} %maximum_select_fusion.3, ...), kind=kOutput, calls=%fused_computation.69 | convolution fusion | flops 4452253696 | bytes 27267072 | tf_op jit(solution)/shard_map/dot_general | solution.py:217
  458.0 9.3 convolution_convert_fusion.2
  472.0 72.3 %reduce-scatter.11.cloned.1.call-done = bf16[512,1024]{1,0:T(8,128)(2,1)} async-done(((bf16[2048,1024]{1,0:T(8,128)(2,1)}), bf16[512,1024]{1,0:T(8,128)(2,1)}) %reduce-scatter.11.cloned.1.call-update) | async-done | bytes 1048592 | tf_op jit(solution)/shard_map/reduce_scatter | solution.py:52
  556.9 81.4 %all-gather.12.cloned.1.call-done = bf16[2048,1024]{1,0:T(8,128)(2,1)} async-done(((bf16[512,1024]{1,0:T(8,128)(2,1)}), bf16[2048,1024]{1,0:T(8,128)(2,1)}) %all-gather.12.cloned.1.call-update) | async-done | bytes 4194320 | tf_op jit(solution)/shard_map/all_gather | solution.py:61
  662.5 75.2 %reduce-scatter.13.cloned.1.call-done = bf16[512,1024]{1,0:T(8,128)(2,1)} async-done(((bf16[2048,1024]{1,0:T(8,128)(2,1)}), bf16[512,1024]{1,0:T(8,128)(2,1)}) %reduce-scatter.13.cloned.1.call-update) | async-done | bytes 1048592 | tf_op jit(solution)/shard_map/reduce_scatter | solution.py:65
  752.8 81.4 %all-gather.14.cloned.1.call-done = bf16[2048,1024]{1,0:T(8,128)(2,1)} async-done(((bf16[512,1024]{1,0:T(8,128)(2,1)}), bf16[2048,1024]{1,0:T(8,128)(2,1)}) %all-gather.14.cloned.1.call-update) | async-done | bytes 4194320 | tf_op jit(solution)/shard_map/all_gather | solution.py:61
  841.0 236.4 %while.33 = (s32[]{:T(128)}, f32[3072,4,64]{0,2,1:T(8,128)}, f32[3072,4,64]{0,2,1:T(8,128)S(1)}, bf16[4,512,4,64]{1,3,2,0:T(8,128)(2,1)}, s32[4]{0:T(128)S(1)}, ...) while((s32[]{:T(128)}, f32[3072,4,64]{0,2,1:T(8,128)}, ...), condition=%wide.region_36.37_spmd, body=%wide.region_34.36_spmd.sunk | while | flops 2073568256 | bytes 215835120 | solution.py:160
  862.7 18.4 %fusion.212 = bf16[4,512,4,64]{1,3,2,0:T(8,128)(2,1)} fusion(bf16[4,512,4,64]{1,3,2,0:T(8,128)(2,1)} %get-tuple-element.686, s32[]{:T(128)S(6)} %copy.78, f32[4,512,1536]{2,1,0:T(8,128)} %fusion.209, f32[4,512,1536]{2,1,0:T(8,128)} %copy-done, pred[512,1536]{1,0:T(8,128)(4,1)} %copy-done.7, bf16[3072,4,64]{0,2,1:T(8,128)(2,1)} %get-tuple-element.711, ...), kind=kOutput, calls=%fused_computation.42.clone.1 | convolution fusion | flops 421662208 | bytes 52428808 | tf_op jit(solution)/shard_map/while/body/eval_jaxpr/hqk,khd->qhd/dot_general | solution.py:145
  881.1 19.2 %fusion.210 = f32[3072,4,64]{0,2,1:T(8,128)} fusion(f32[3072,4,64]{0,2,1:T(8,128)} %get-tuple-element.684, s32[]{:T(128)S(6)} %select_n.270, f32[4,512,1536]{2,1,0:T(8,128)} %fusion.209, f32[4,512,1536]{2,1,0:T(8,128)} %copy-done, pred[512,1536]{1,0:T(8,128)(4,1)} %copy-done.7, bf16[2048,4,64]{0,2,1:T(8,128)(2,1)} %get-tuple-element.708, ...), kind=kOutput, calls=%fused_computation.36.clone.1 | convolution fusion | flops 422317568 | bytes 54525960 | tf_op jit(solution)/shard_map/while/body/eval_jaxpr/hqk,qhd->khd/dot_general | solution.py:149
  921.8 18.3 %fusion.212 = bf16[4,512,4,64]{1,3,2,0:T(8,128)(2,1)} fusion(bf16[4,512,4,64]{1,3,2,0:T(8,128)(2,1)} %get-tuple-element.686, s32[]{:T(128)S(6)} %copy.78, f32[4,512,1536]{2,1,0:T(8,128)} %fusion.209, f32[4,512,1536]{2,1,0:T(8,128)} %copy-done, pred[512,1536]{1,0:T(8,128)(4,1)} %copy-done.7, bf16[3072,4,64]{0,2,1:T(8,128)(2,1)} %get-tuple-element.711, ...), kind=kOutput, calls=%fused_computation.42.clone.1 | convolution fusion | flops 421662208 | bytes 52428808 | tf_op jit(solution)/shard_map/while/body/eval_jaxpr/hqk,khd->qhd/dot_general | solution.py:145
  940.2 19.2 %fusion.210 = f32[3072,4,64]{0,2,1:T(8,128)} fusion(f32[3072,4,64]{0,2,1:T(8,128)} %get-tuple-element.684, s32[]{:T(128)S(6)} %select_n.270, f32[4,512,1536]{2,1,0:T(8,128)} %fusion.209, f32[4,512,1536]{2,1,0:T(8,128)} %copy-done, pred[512,1536]{1,0:T(8,128)(4,1)} %copy-done.7, bf16[2048,4,64]{0,2,1:T(8,128)(2,1)} %get-tuple-element.708, ...), kind=kOutput, calls=%fused_computation.36.clone.1 | convolution fusion | flops 422317568 | bytes 54525960 | tf_op jit(solution)/shard_map/while/body/eval_jaxpr/hqk,qhd->khd/dot_general | solution.py:149
  980.9 18.3 %fusion.212 = bf16[4,512,4,64]{1,3,2,0:T(8,128)(2,1)} fusion(bf16[4,512,4,64]{1,3,2,0:T(8,128)(2,1)} %get-tuple-element.686, s32[]{:T(128)S(6)} %copy.78, f32[4,512,1536]{2,1,0:T(8,128)} %fusion.209, f32[4,512,1536]{2,1,0:T(8,128)} %copy-done, pred[512,1536]{1,0:T(8,128)(4,1)} %copy-done.7, bf16[3072,4,64]{0,2,1:T(8,128)(2,1)} %get-tuple-element.711, ...), kind=kOutput, calls=%fused_computation.42.clone.1 | convolution fusion | flops 421662208 | bytes 52428808 | tf_op jit(solution)/shard_map/while/body/eval_jaxpr/hqk,khd->qhd/dot_general | solution.py:145
  999.2 19.2 %fusion.210 = f32[3072,4,64]{0,2,1:T(8,128)} fusion(f32[3072,4,64]{0,2,1:T(8,128)} %get-tuple-element.684, s32[]{:T(128)S(6)} %select_n.270, f32[4,512,1536]{2,1,0:T(8,128)} %fusion.209, f32[4,512,1536]{2,1,0:T(8,128)} %copy-done, pred[512,1536]{1,0:T(8,128)(4,1)} %copy-done.7, bf16[2048,4,64]{0,2,1:T(8,128)(2,1)} %get-tuple-element.708, ...), kind=kOutput, calls=%fused_computation.36.clone.1 | convolution fusion | flops 422317568 | bytes 54525960 | tf_op jit(solution)/shard_map/while/body/eval_jaxpr/hqk,qhd->khd/dot_general | solution.py:149
  1039.9 18.2 %fusion.212 = bf16[4,512,4,64]{1,3,2,0:T(8,128)(2,1)} fusion(bf16[4,512,4,64]{1,3,2,0:T(8,128)(2,1)} %get-tuple-element.686, s32[]{:T(128)S(6)} %copy.78, f32[4,512,1536]{2,1,0:T(8,128)} %fusion.209, f32[4,512,1536]{2,1,0:T(8,128)} %copy-done, pred[512,1536]{1,0:T(8,128)(4,1)} %copy-done.7, bf16[3072,4,64]{0,2,1:T(8,128)(2,1)} %get-tuple-element.711, ...), kind=kOutput, calls=%fused_computation.42.clone.1 | convolution fusion | flops 421662208 | bytes 52428808 | tf_op jit(solution)/shard_map/while/body/eval_jaxpr/hqk,khd->qhd/dot_general | solution.py:145
  1058.1 19.3 %fusion.210 = f32[3072,4,64]{0,2,1:T(8,128)} fusion(f32[3072,4,64]{0,2,1:T(8,128)} %get-tuple-element.684, s32[]{:T(128)S(6)} %select_n.270, f32[4,512,1536]{2,1,0:T(8,128)} %fusion.209, f32[4,512,1536]{2,1,0:T(8,128)} %copy-done, pred[512,1536]{1,0:T(8,128)(4,1)} %copy-done.7, bf16[2048,4,64]{0,2,1:T(8,128)(2,1)} %get-tuple-element.708, ...), kind=kOutput, calls=%fused_computation.36.clone.1 | convolution fusion | flops 422317568 | bytes 54525960 | tf_op jit(solution)/shard_map/while/body/eval_jaxpr/hqk,qhd->khd/dot_general | solution.py:149
  1109.8 10.0 fusion.158
  1120.0 11.5 fusion.132
  1141.2 35.2 %reduce-scatter.15.cloned.1.call-done = bf16[512,1024]{1,0:T(8,128)(2,1)} async-done(((bf16[2048,1024]{1,0:T(8,128)(2,1)}), bf16[512,1024]{1,0:T(8,128)(2,1)}) %reduce-scatter.15.cloned.1.call-update) | async-done | bytes 1048592 | tf_op jit(solution)/shard_map/reduce_scatter | solution.py:65
  1191.0 20.4 %all-reduce.4 = (f32[2,256]{1,0:T(2,128)}, f32[1024]{0:T(1024)}) all-reduce(f32[2,256]{1,0:T(2,128)S(1)} %pad_maximum_fusion.3, f32[1024]{0:T(1024)S(1)} %copy-done.51), channel_id=1, replica_groups=mesh['dp'=8,'tensor'=4] {'dp'}, use_global_device_ids=true, to_apply=%region_48.49 | all-reduce | flops 1536 | bytes 12288 | tf_op jit(solution)/shard_map/psum | solution.py:291
  1211.3 15.4 %reduce-scatter.17.cloned.1.call-done = f32[3,128,256]{1,2,0:T(8,128)} async-done(((f32[3,1024,256]{1,2,0:T(8,128)}), f32[3,128,256]{1,2,0:T(8,128)}) %reduce-scatter.17.cloned.1.call-update) | async-done | bytes 393232 | tf_op jit(solution)/shard_map/reduce_scatter | solution.py:286
  1228.7 40.5 %all-reduce.3 = (f32[1024]{0:T(1024)}, f32[1024]{0:T(1024)}, f32[4,1024]{1,0:T(4,128)}, f32[4,1024]{1,0:T(4,128)}) all-reduce(f32[1024]{0:T(1024)S(1)} %copy-done.58, f32[1024]{0:T(1024)S(1)} %copy-done.57, f32[4,1024]{1,0:T(4,128)S(1)} %get-tuple-element.461, ...), channel_id=1, replica_groups=mesh['dp'=8,'tensor'=4] {'dp','tensor'}, use_global_device_ids=true, to_apply=%region_50.51 | all-reduce | flops 10240 | bytes 81920 | tf_op jit(solution)/shard_map/psum | solution.py:294
  1269.2 13.6 reduce-scatter.23.cloned.1.call-done
  1282.8 55.1 %reduce-scatter.21.cloned.1.call-done = f32[128,1024]{1,0:T(8,128)} async-done(((f32[1024,1024]{1,0:T(8,128)}), f32[128,1024]{1,0:T(8,128)}) %reduce-scatter.21.cloned.1.call-update) | async-done | bytes 524304 | tf_op jit(solution)/shard_map/reduce_scatter | solution.py:288
  1338.0 40.2 %reduce-scatter.19.cloned.1.call-done = f32[256,128]{1,0:T(8,128)} async-done(((f32[256,1024]{1,0:T(8,128)}), f32[256,128]{1,0:T(8,128)}) %reduce-scatter.19.cloned.1.call-update) | async-done | bytes 131088 | tf_op jit(solution)/shard_map/reduce_scatter | solution.py:287
  (387 shorter events, 306.2 us)
Async XLA Ops:
  7.2 20.7 %all-to-all-start = ((bf16[8,64,1024]{2,1,0:T(8,128)(2,1)}), bf16[8,64,1024]{2,1,0:T(8,128)(2,1)S(1)}, u32[]{:S(2)}, u32[]{:S(2)}) async-start(bf16[8,64,1024]{2,1,0:T(8,128)(2,1)} %bitcast.172), calls=%async_computation | async-start | bytes 2097152 | tf_op jit(solution)/shard_map/all_to_all | solution.py:175
  12.5 61.0 %all-gather.6.cloned.1.call-start = ((), (), s32[]{:S(2)}) async-start(), calls=%async_computation.12 | async-start | bytes 1769472 | tf_op jit(solution)/shard_map/all_gather | solution.py:189
  32.6 22.2 %collective-permute-start = (bf16[512,1024]{1,0:T(8,128)(2,1)S(1)}, bf16[512,1024]{1,0:T(8,128)(2,1)S(1)}, u32[]{:S(2)}, u32[]{:S(2)}) collective-permute-start(bf16[512,1024]{1,0:T(8,128)(2,1)S(1)} %add_convert_fusion.5), channel_id=1, source_target_pairs={{0,1},{1,0},{2,3},{3,2},{4,5},{5,4},{6,7},{7,6},{8,9},{9,8},{10,11... | collective-permute-start | bytes 3145736 | tf_op jit(solution)/shard_map/ppermute | solution.py:20
  35.1 268.3 %reduce-scatter.9.cloned.1.call-start = ((), (), s32[]{:S(2)}) async-start(), calls=%async_computation.13 | async-start | bytes 5242880 | tf_op jit(solution)/shard_map/reduce_scatter | solution.py:52
  57.2 89.7 %collective-permute-start.1 = (bf16[1024,1024]{1,0:T(8,128)(2,1)}, bf16[1024,1024]{1,0:T(8,128)(2,1)S(1)}, u32[]{:S(2)}, u32[]{:S(2)}) collective-permute-start(bf16[1024,1024]{1,0:T(8,128)(2,1)} %maximum_select_fusion.2), channel_id=1, source_target_pairs={{0,2},{1,3},{2,0},{3,1},{4,6},{5,7},{6,4},{7,5},{8,10},{9,11},{10,... | collective-permute-start | bytes 6291464 | tf_op jit(solution)/shard_map/ppermute | solution.py:20
  221.1 82.4 %copy-start.26 = (f32[1024]{0:T(1024)S(1)}, f32[1024]{0:T(1024)}, u32[]{:S(2)}) copy-start(f32[1024]{0:T(1024)} %param.27) | copy-start | bytes 12292
  221.1 86.2 %copy-start.2 = (bf16[8,64,1024]{2,1,0:T(8,128)(2,1)S(1)}, bf16[8,64,1024]{2,1,0:T(8,128)(2,1)}, u32[]{:S(2)}) copy-start(bf16[8,64,1024]{2,1,0:T(8,128)(2,1)} %copy-done.1) | copy-start | bytes 3145732
  221.1 86.2 %copy-start.35 = (f32[1,1024]{1,0:T(1,128)S(1)}, f32[1,1024]{1,0:T(1,128)}, u32[]{:S(2)}) copy-start(f32[1,1024]{1,0:T(1,128)} %get-tuple-element.445) | copy-start | bytes 12292
  221.1 86.2 %copy-start.54 = (f32[1,1024]{1,0:T(1,128)S(1)}, f32[1,1024]{1,0:T(1,128)}, u32[]{:S(2)}) copy-start(f32[1,1024]{1,0:T(1,128)} %get-tuple-element.449) | copy-start | bytes 12292
  221.1 118.9 %all-gather.8.cloned.1.call-start = ((), (), s32[]{:S(2)}) async-start(), calls=%async_computation.14 | async-start | bytes 2359296 | tf_op jit(solution)/shard_map/all_gather | solution.py:214
  221.9 236.1 %all-gather.10.cloned.1.call-start = ((), (), s32[]{:S(2)}) async-start(), calls=%async_computation.15 | async-start | bytes 2359296 | tf_op jit(solution)/shard_map/all_gather | solution.py:215
  309.6 120.4 %copy-start.60 = (f32[1024]{0:T(1024)S(1)}, f32[1024]{0:T(1024)}, u32[]{:S(2)}) copy-start(f32[1024]{0:T(1024)} %param.28) | copy-start | bytes 12292
  309.6 25.0 %collective-permute-start.2 = (bf16[512,1024]{1,0:T(8,128)(2,1)S(1)}, bf16[512,1024]{1,0:T(8,128)(2,1)S(1)}, u32[]{:S(2)}, u32[]{:S(2)}) collective-permute-start(bf16[512,1024]{1,0:T(8,128)(2,1)S(1)} %add_convert_fusion.2), channel_id=1, source_target_pairs={{0,1},{1,0},{2,3},{3,2},{4,5},{5,4},{6,7},{7,6},{8,9},{9,8},{10,11... | collective-permute-start | bytes 3145736 | tf_op jit(solution)/shard_map/ppermute | solution.py:20
  336.9 93.0 %collective-permute-start.3 = (bf16[1024,1024]{1,0:T(8,128)(2,1)}, bf16[1024,1024]{1,0:T(8,128)(2,1)}, u32[]{:S(2)}, u32[]{:S(2)}) collective-permute-start(bf16[1024,1024]{1,0:T(8,128)(2,1)} %maximum_select_fusion.3), channel_id=1, source_target_pairs={{0,2},{1,3},{2,0},{3,1},{4,6},{5,7},{6,4},{7,5},{8,10},{9,11},{10,... | collective-permute-start | bytes 6291464 | tf_op jit(solution)/shard_map/ppermute | solution.py:20
  339.9 204.5 %reduce-scatter.11.cloned.1.call-start = ((), (), s32[]{:S(2)}) async-start(), calls=%async_computation.16 | async-start | bytes 5242880 | tf_op jit(solution)/shard_map/reduce_scatter | solution.py:52
  467.3 77.1 %copy-start.27 = (f32[1024]{0:T(1024)S(1)}, f32[1024]{0:T(1024)}, u32[]{:S(2)}) copy-start(f32[1024]{0:T(1024)} %param.29) | copy-start | bytes 12292
  467.3 80.9 %all-to-all-start.2 = ((bf16[8,64,1024]{2,1,0:T(8,128)(2,1)}), bf16[8,64,1024]{2,1,0:T(8,128)(2,1)}, u32[]{:S(2)}, u32[]{:S(2)}) async-start(bf16[8,64,1024]{2,1,0:T(8,128)(2,1)} %bitcast.31), calls=%async_computation.4 | async-start | bytes 2097152 | tf_op jit(solution)/shard_map/all_to_all | solution.py:176
  471.6 76.6 %copy-start.37 = (f32[1,1024]{1,0:T(1,128)S(1)}, f32[1,1024]{1,0:T(1,128)}, u32[]{:S(2)}) copy-start(f32[1,1024]{1,0:T(1,128)} %get-tuple-element.447) | copy-start | bytes 12292
  471.6 166.7 %all-gather.12.cloned.1.call-start = ((), (), s32[]{:S(2)}) async-start(), calls=%async_computation.17 | async-start | bytes 5242880 | tf_op jit(solution)/shard_map/all_gather | solution.py:61
  556.9 180.9 %reduce-scatter.13.cloned.1.call-start = ((), (), s32[]{:S(2)}) async-start(), calls=%async_computation.18 | async-start | bytes 5242880 | tf_op jit(solution)/shard_map/reduce_scatter | solution.py:65
  662.3 171.9 %all-gather.14.cloned.1.call-start = ((), (), s32[]{:S(2)}) async-start(), calls=%async_computation.19 | async-start | bytes 5242880 | tf_op jit(solution)/shard_map/all_gather | solution.py:61
  750.1 84.1 %copy-start.25 = (bf16[256,1024]{1,0:T(8,128)(2,1)S(1)}, bf16[256,1024]{1,0:T(8,128)(2,1)}, u32[]{:S(2)}) copy-start(bf16[256,1024]{1,0:T(8,128)(2,1)} %all_gather.23) | copy-start | bytes 1572868
  752.8 423.6 %reduce-scatter.15.cloned.1.call-start = ((), (), s32[]{:S(2)}) async-start(), calls=%async_computation.20 | async-start | bytes 5242880 | tf_op jit(solution)/shard_map/reduce_scatter | solution.py:65
  1100.9 125.8 %reduce-scatter.17.cloned.1.call-start = ((), (), s32[]{:S(2)}) async-start(), calls=%async_computation.21 | async-start | bytes 3538944 | tf_op jit(solution)/shard_map/reduce_scatter | solution.py:286
  1109.8 173.1 %reduce-scatter.23.cloned.1.call-start = ((), (), s32[]{:S(2)}) async-start(), calls=%async_computation.24 | async-start | bytes 4718592 | tf_op jit(solution)/shard_map/reduce_scatter | solution.py:289
  1119.8 218.2 %reduce-scatter.21.cloned.1.call-start = ((), (), s32[]{:S(2)}) async-start(), calls=%async_computation.23 | async-start | bytes 4718592 | tf_op jit(solution)/shard_map/reduce_scatter | solution.py:288
  1132.3 51.6 %all-to-all-start.1 = ((bf16[8,64,1024]{2,1,0:T(8,128)(2,1)}), bf16[8,64,1024]{2,1,0:T(8,128)(2,1)}, u32[]{:S(2)}, u32[]{:S(2)}) async-start(bf16[8,64,1024]{2,1,0:T(8,128)(2,1)} %bitcast.29), calls=%async_computation.3 | async-start | bytes 2097152 | tf_op jit(solution)/shard_map/all_to_all | solution.py:298
  1136.5 39.8 %copy-start.3 = (bf16[8,64,1024]{2,1,0:T(8,128)(2,1)S(1)}, bf16[8,64,1024]{2,1,0:T(8,128)(2,1)}, u32[]{:S(2)}) copy-start(bf16[8,64,1024]{2,1,0:T(8,128)(2,1)} %copy-done.1) | copy-start | bytes 3145732
  1136.5 39.8 %copy-start.30 = (f32[1,1024]{1,0:T(1,128)S(1)}, f32[1,1024]{1,0:T(1,128)}, u32[]{:S(2)}) copy-start(f32[1,1024]{1,0:T(1,128)} %copy-done.29) | copy-start | bytes 12292
  1136.6 39.8 %copy-start.32 = (f32[512]{0:T(512)S(1)}, f32[512]{0:T(512)}, u32[]{:S(2)}) copy-start(f32[512]{0:T(512)} %copy-done.31) | copy-start | bytes 6148
  1136.6 241.6 %reduce-scatter.19.cloned.1.call-start = ((), (), s32[]{:S(2)}) async-start(), calls=%async_computation.22 | async-start | bytes 1179648 | tf_op jit(solution)/shard_map/reduce_scatter | solution.py:287
  1183.9 85.3 %all-to-all-start.3 = ((bf16[8,64,1024]{2,1,0:T(8,128)(2,1)}), bf16[8,64,1024]{2,1,0:T(8,128)(2,1)}, u32[]{:S(2)}, u32[]{:S(2)}) async-start(bf16[8,64,1024]{2,1,0:T(8,128)(2,1)} %bitcast.167), calls=%async_computation.7 | async-start | bytes 2097152 | tf_op jit(solution)/shard_map/all_to_all | solution.py:299
  (67 other events, 714.5 us)
Sparse Core Ops, SparseCore 0:
  35.2 24.2 all-gather.5
  221.2 82.1 reduce-scatter.8
  305.5 28.3 all-gather.7
  340.0 26.6 all-gather.9
  467.4 76.8 reduce-scatter.10
  557.0 81.2 all-gather.11
  662.4 75.2 reduce-scatter.12
  752.9 81.2 all-gather.13
  1101.0 75.2 reduce-scatter.14
  1179.6 47.0 reduce-scatter.16
  1231.0 51.7 reduce-scatter.22
  1286.6 51.3 reduce-scatter.20
  1342.0 36.0 reduce-scatter.18
